TPU v7x, 512 devices: a whole 4x8x8 slice. The times are simulated.
512 devices in a mesh: seq: 64 (over y, x, core), head: 8 (over z).
Axes of the slice: x: 4, y: 8, z: 8, core: 2. Of those that a mesh axis runs over, the one named last changes fastest.
Arguments:
- hidden_states: bfloat16 [49152, 8192], P('seq', 'head'), may hold values from -6 to 6
- k_weight: bfloat16 [8192, 1024], P('head', 'seq'), may hold values from -0.0625 to 0.0625
- v_weight: bfloat16 [8192, 1024], P('head', 'seq'), may hold values from -0.0625 to 0.0625
- assignments: int32 [8, 49152], P('head', 'seq'), may hold values from 0 to 1023
- old_centroids: float32 [8, 1024, 128], P('head'), may hold values from -6 to 6
Outputs:
- key_cache: bfloat16 [49152, 1024], P('seq', 'head')
- value_cache: bfloat16 [49152, 1024], P('seq', 'head')
- new_centroids: float32 [8, 1024, 128], P('head', 'seq')
- distances: bfloat16 [8, 49152, 1024], P('head', 'seq')
All inputs are finite; a program needn't handle non-finite values.
Results may differ from a plain program's by a relative error of at most 0.017.
Values may be sent and summed in bfloat16 or wider, within the bound.
A program may use at most 64 MiB of HBM per device.

v0:
```python
import jax
import jax.numpy as jnp
from jax import lax
from jax.sharding import PartitionSpec as P


def shards(hidden_states, k_weight, v_weight, assignments, old_centroids):
    tok_rows = hidden_states.shape[0]
    heads_local = old_centroids.shape[0]
    clusters = old_centroids.shape[1]
    head_size = old_centroids.shape[2]
    stacked = jnp.stack((k_weight, v_weight), axis=1)
    partial_terms = jnp.einsum(
        "td,dkc->tkc",
        hidden_states,
        lax.all_gather(stacked, "seq", axis=2, tiled=True),
        preferred_element_type=jnp.float32,
    )
    summed = lax.psum_scatter(
        partial_terms.astype(jnp.bfloat16), "head", scatter_dimension=2, tiled=True
    ).astype(jnp.float32)
    key_cache = summed[:, 0].astype(jnp.bfloat16)
    value_cache = summed[:, 1].astype(jnp.bfloat16)
    key_heads = key_cache.reshape(tok_rows, heads_local, head_size)
    onehot = (
        assignments[:, :, None] == jnp.arange(clusters, dtype=jnp.int32)[None, None, :]
    ).astype(jnp.bfloat16)
    local_sums = jnp.einsum("htc,the->che", onehot, key_heads, preferred_element_type=jnp.float32)
    local_counts = jnp.swapaxes(jnp.sum(onehot, axis=1, dtype=jnp.float32), 0, 1)
    prior_weight = float(tok_rows * lax.axis_size("seq") // clusters)
    old_turned = jnp.swapaxes(old_centroids, 0, 1)
    share_rows = clusters // lax.axis_size("seq")
    first_row = lax.axis_index("seq") * share_rows
    total_sums, total_counts = lax.psum((local_sums, local_counts), "seq")
    updated = (total_sums + prior_weight * old_turned) / (total_counts[:, :, None] + prior_weight)
    centroid_low = updated.astype(jnp.bfloat16)
    own_rows = lax.dynamic_slice_in_dim(updated, first_row, share_rows, 0)
    new_centroids = jnp.swapaxes(own_rows, 0, 1)
    centroid_wide = centroid_low.astype(jnp.float32)
    centroid_square = jnp.swapaxes(jnp.sum(centroid_wide * centroid_wide, axis=2), 0, 1)
    key_wide = key_heads.astype(jnp.float32)
    key_square = jnp.swapaxes(jnp.sum(key_wide * key_wide, axis=2), 0, 1)
    cross_term = jnp.einsum(
        "the,che->htc", key_heads, centroid_low, preferred_element_type=jnp.float32
    )
    dist = (key_square[:, :, None] - 2.0 * cross_term + centroid_square[:, None, :]) / head_size
    return (key_cache, value_cache, new_centroids, dist.astype(jnp.bfloat16))


def solution(mesh):
    in_specs = (
        P("seq", "head"),
        P("head", "seq"),
        P("head", "seq"),
        P("head", "seq"),
        P("head", None, None),
    )
    out_specs = (P("seq", "head"), P("seq", "head"), P("head", "seq", None), P("head", "seq", None))
    return jax.shard_map(shards, mesh=mesh, in_specs=in_specs, out_specs=out_specs, check_vma=False)
```

profile of v0, /device:TPU:1, one launch (start us, length us, event | category | flops | bytes accessed | tf_op | source)
XLA Modules:
  0.0 438.5 jit_solution(4969922273733050903)
XLA Ops:
  7.2 0.0 copy-start
  7.2 0.0 all-gather.2.cloned.1.call-start
  7.2 1.5 pad_maximum_fusion
  8.7 0.0 all-gather.2.cloned.1.call-update
  8.8 0.0 reduce-scatter.2.cloned.1.call-start
  8.8 93.4 %all-gather.2.cloned.1.call-done = bf16[1024,2,1024]{0,2,1:T(8,128)(2,1)} async-done(((bf16[1024,2,16]{0,2,1:T(8,128)(2,1)}), bf16[1024,2,1024]{0,2,1:T(8,128)(2,1)}) %all-gather.2.cloned.1.call-update) | async-done | bytes 4194320 | tf_op jit(solution)/shard_map/all_gather | solution.py:16
  102.3 0.0 copy-done
  102.3 7.4 %convert_bitcast_fusion = bf16[768,2,1024]{0,2,1:T(8,128)(2,1)} fusion(bf16[1024,2,1024]{0,2,1:T(8,128)(2,1)} %all-gather.2.cloned.1.call-done, bf16[768,1024]{1,0:T(8,128)(2,1)S(1)} %copy-done), kind=kOutput, calls=%fused_computation.4 | convolution fusion | flops 3222798336 | bytes 8912896 | tf_op jit(solution)/shard_map/td,dkc->tkc/dot_general | solution.py:13
  109.6 0.0 copy-start.2
  109.6 0.0 copy-start.3
  109.6 0.0 reduce-scatter.2.cloned.1.call-update
  109.7 0.0 all-reduce.2.cloned.1.call-start
  109.7 1.0 copy-done.2
  110.7 0.2 copy.16
  110.9 0.0 copy-done.3
  110.9 0.4 convert_reduce_fusion
  111.3 123.7 %psum.15 = f32[1024,1]{0,1:T(1,128)S(1)} all-reduce(f32[1024,1]{0,1:T(1,128)S(1)} %bitcast.40), channel_id=1, replica_groups=mesh['seq'=64,'head'=8] {'seq'}, use_global_device_ids=true, to_apply=%region_3.0 | all-reduce | flops 1024 | bytes 8192 | tf_op jit(solution)/shard_map/psum | solution.py:34
  235.0 0.0 reduce-scatter.2.cloned.1.call-done
  235.0 0.0 copy-start.1
  235.0 2.6 fusion.7
  237.6 0.0 all-reduce.2.cloned.1.call-update
  237.7 1.0 slice_bitcast_fusion
  238.7 0.8 copy.18
  239.5 0.8 copy.19
  240.3 0.0 copy-done.1
  240.3 0.1 multiply_reduce_fusion.1
  240.4 187.8 %all-reduce.2.cloned.1.call-done = f32[1024,1,128]{0,2,1:T(8,128)} async-done(((f32[1024,1,128]{0,2,1:T(8,128)}), f32[1024,1,128]{0,2,1:T(8,128)}) %all-reduce.2.cloned.1.call-update) | async-done | bytes 524304 | tf_op jit(solution)/shard_map/psum | solution.py:34
  428.2 1.2 multiply_reduce_fusion
  429.4 0.1 constant_dynamic-slice_fusion
  429.5 0.7 copy.17
  430.2 1.8 fusion.6
  (2 shorter events, 0.0 us)
Async XLA Ops:
  7.2 95.1 %copy-start = (bf16[768,1024]{1,0:T(8,128)(2,1)S(1)}, bf16[768,1024]{1,0:T(8,128)(2,1)}, u32[]{:S(2)}) copy-start(bf16[768,1024]{1,0:T(8,128)(2,1)} %param.5) | copy-start | bytes 4718596
  7.2 95.1 %all-gather.2.cloned.1.call-start = ((), (), s32[]{:S(2)}) async-start(), calls=%async_computation.1 | async-start | bytes 4259840 | tf_op jit(solution)/shard_map/all_gather | solution.py:16
  8.8 226.2 %reduce-scatter.2.cloned.1.call-start = ((), (), s32[]{:S(2)}) async-start(), calls=%async_computation.2 | async-start | bytes 3538944 | tf_op jit(solution)/shard_map/reduce_scatter | solution.py:19
  109.6 1.0 copy-start.2
  109.6 1.2 copy-start.3
  109.7 318.6 %all-reduce.2.cloned.1.call-start = ((), (), s32[]{:S(2)}) async-start(), calls=%async_computation.3 | async-start | bytes 1048576 | tf_op jit(solution)/shard_map/psum | solution.py:34
  235.0 5.3 %copy-start.1 = (bf16[768,2,128]{0,2,1:T(8,128)(2,1)S(1)}, bf16[768,2,128]{0,2,1:T(8,128)(2,1)}, u32[]{:S(2)}) copy-start(bf16[768,2,128]{0,2,1:T(8,128)(2,1)} %reduce-scatter.2.cloned.1.call-done) | copy-start | bytes 1179652
Sparse Core Ops, SparseCore 0:
  12.0 90.2 all-gather.1
  109.8 44.7 reduce-scatter.1
  237.8 190.4 all-reduce.1
where the time goes:
time: 439 us
  waiting for transfers between devices  281 us (64%)
  blocking collectives  124 us (28%)
  between operations  13.8 us (3%)
  matrix products  11.8 us (3%)
  local copies, waits for them, and re-layouts  4.61 us (1%)
    psum x1, waiting for transfers between devices, shards(): total_sums, total_counts = lax.psum((local_sums, local_counts), 'seq')  188 us
    psum x1, blocking collectives, shards(): total_sums, total_counts = lax.psum((local_sums, local_counts), 'seq')  124 us
    all_gather x1, waiting for transfers between devices, shards(): lax.all_gather(stacked, 'seq', axis=2, tiled=True)  93.4 us
  transfers between devices with their start and end apart: 3, of which 2 were waited for; matrix products, arithmetic and copies ran while one was open for 1% of the time, Pallas kernels for 0%

commit v1 on v0

v1 whole, which is shorter than its diff:
```python
import jax
import jax.numpy as jnp
from jax import lax
from jax.experimental import pallas as pl
from jax.experimental.pallas import tpu as pltpu
from jax.sharding import PartitionSpec as P

MESH = pl.DeviceIdType.MESH


def centroid_kernel(
    n, prior, sums_ref, cnt_ref, old_ref, new_ref, low_ref, got, got_cnt, low, send_sem, recv_sem
):
    me = lax.axis_index("seq")

    def peer(d):
        return {"seq": lax.rem(me + d, n)}

    barrier = pltpu.get_barrier_semaphore()

    def greet(d, c):
        pl.semaphore_signal(barrier, inc=1, device_id=peer(d), device_id_type=MESH)
        return c

    lax.fori_loop(1, n, greet, 0)
    pl.semaphore_wait(barrier, n - 1)

    def copy(src, dst, k, d):
        return pltpu.make_async_remote_copy(
            src_ref=src, dst_ref=dst, send_sem=send_sem.at[k], recv_sem=recv_sem.at[k],
            device_id=peer(d), device_id_type=MESH,
        )

    def scatter(d, c):
        to = lax.rem(me + d, n)
        copy(sums_ref.at[to], got.at[d - 1], 0, d).start()
        copy(cnt_ref.at[to], got_cnt.at[d - 1], 1, d).start()
        return c

    lax.fori_loop(1, n, scatter, 0)
    copy(got, got, 0, 1).wait_recv()
    copy(got_cnt, got_cnt, 1, 1).wait_recv()

    def add(i, c):
        return c[0] + got[i], c[1] + got_cnt[i]

    total, cnt = lax.fori_loop(0, n - 1, add, (sums_ref[me], cnt_ref[me]))
    rows = total.shape[0]
    lane = lax.broadcasted_iota(jnp.int32, (rows, 128), 1)
    row = lax.broadcasted_iota(jnp.int32, (rows, 128), 0)
    count = jnp.sum(
        jnp.where(lane == row, jnp.broadcast_to(cnt, (rows, 128)), 0.0), axis=1, keepdims=True
    )
    new = (total + prior * old_ref[...]) / (count + prior)
    new_ref[...] = new
    low[me] = new.astype(jnp.bfloat16)

    def gather(d, c):
        copy(low.at[me], low.at[me], 2, d).start()
        return c

    lax.fori_loop(1, n, gather, 0)
    rest = low.at[pl.ds(0, n - 1)]
    copy(rest, rest, 2, 1).wait_recv()
    low_ref[...] = low[...]
    copy(got, got, 0, 1).wait_send()
    copy(got_cnt, got_cnt, 1, 1).wait_send()
    copy(rest, rest, 2, 1).wait_send()


def update_centroids(sums, counts, old_own, prior):
    n, rows, width = sums.shape
    vmem = pl.BlockSpec(memory_space=pltpu.VMEM)

    def body(*refs):
        centroid_kernel(n, prior, *refs)

    return pl.pallas_call(
        body,
        name="centroids",
        out_shape=(
            jax.ShapeDtypeStruct((rows, width), jnp.float32),
            jax.ShapeDtypeStruct((n, rows, width), jnp.bfloat16),
        ),
        in_specs=[vmem] * 3,
        out_specs=(vmem, vmem),
        scratch_shapes=[
            pltpu.VMEM((n - 1, rows, width), jnp.float32),
            pltpu.VMEM((n - 1, 1, 128), jnp.float32),
            pltpu.VMEM((n, rows, width), jnp.bfloat16),
            pltpu.SemaphoreType.DMA((3,)),
            pltpu.SemaphoreType.DMA((3,)),
        ],
        compiler_params=pltpu.CompilerParams(collective_id=0, has_side_effects=True),
    )(sums, counts, old_own)


def shards(hidden_states, k_weight, v_weight, assignments, old_centroids):
    tok_rows = hidden_states.shape[0]
    clusters = old_centroids.shape[1]
    head_size = old_centroids.shape[2]
    n_seq = lax.axis_size("seq")
    stacked = jnp.stack((k_weight, v_weight), axis=1)
    partial_terms = jnp.einsum(
        "td,dkc->tkc",
        hidden_states,
        lax.all_gather(stacked, "seq", axis=2, tiled=True),
        preferred_element_type=jnp.float32,
    )
    summed = lax.psum_scatter(
        partial_terms.astype(jnp.bfloat16), "head", scatter_dimension=2, tiled=True
    ).astype(jnp.float32)
    keys = summed[:, 0].astype(jnp.bfloat16)
    value_cache = summed[:, 1].astype(jnp.bfloat16)
    onehot = assignments[0][:, None] == jnp.arange(clusters, dtype=jnp.int32)[None, :]
    local_sums = jnp.einsum(
        "tc,te->ce", onehot.astype(jnp.bfloat16), keys, preferred_element_type=jnp.float32
    )
    local_counts = jnp.sum(onehot.astype(jnp.float32), axis=0)
    prior_weight = float(tok_rows * n_seq // clusters)
    share = clusters // n_seq
    counts = jnp.pad(local_counts.reshape(n_seq, 1, share), ((0, 0), (0, 0), (0, 128 - share)))
    old_own = lax.dynamic_slice_in_dim(old_centroids[0], lax.axis_index("seq") * share, share, 0)
    new_own, low = update_centroids(
        local_sums.reshape(n_seq, share, head_size), counts, old_own, prior_weight
    )
    low = low.reshape(clusters, head_size)
    wide = low.astype(jnp.float32)
    centroid_square = jnp.sum(wide * wide, axis=1)
    key_wide = keys.astype(jnp.float32)
    key_square = jnp.sum(key_wide * key_wide, axis=1)
    cross_term = jnp.einsum("te,ce->tc", keys, low, preferred_element_type=jnp.float32)
    dist = (key_square[:, None] - 2.0 * cross_term + centroid_square[None, :]) / head_size
    return (keys, value_cache, new_own[None], dist.astype(jnp.bfloat16)[None])


def solution(mesh):
    in_specs = (
        P("seq", "head"),
        P("head", "seq"),
        P("head", "seq"),
        P("head", "seq"),
        P("head", None, None),
    )
    out_specs = (P("seq", "head"), P("seq", "head"), P("head", "seq", None), P("head", "seq", None))
    return jax.shard_map(shards, mesh=mesh, in_specs=in_specs, out_specs=out_specs, check_vma=False)
```

time: 439 us -> 210 us (0.48)
  waiting for transfers between devices: 281 us -> 135 us
  blocking collectives: 124 us -> 0 us
  Pallas kernels: 0 us -> 38.7 us
    psum x1 -> x0, waiting for transfers between devices: 188 us -> none  [shards(): total_sums, total_counts = lax.psum((local_sums, local_counts), 'seq')]
    psum x1 -> x0, blocking collectives: 124 us -> none  [shards(): total_sums, total_counts = lax.psum((local_sums, local_counts), 'seq')]
    reduce_scatter x1, waiting for transfers between devices: 0.01 us -> 41.9 us  [shards(): lax.psum_scatter(partial_terms.astype(jnp.bfloat16), 'head', scatter_dime...]
    pallas_call x0 -> x1, Pallas kernels: none -> 38.7 us  [update_centroids(): pl.pallas_call(body, name='centroids', out_shape=(jax.ShapeDtypeStruct((r...]
  transfers between devices with their start and end apart: 3 -> 2, of which waited for: 2 -> 2; matrix products, arithmetic and copies ran while one was open for 1% -> 1% of each run, Pallas kernels for 0% -> 0%
where the time goes in v1:
time: 210 us
  waiting for transfers between devices  135 us (64%)
  Pallas kernels  38.7 us (18%)
  between operations  14.1 us (7%)
  matrix products  12.6 us (6%)
  local copies, waits for them, and re-layouts  6.07 us (3%)
  other arithmetic  3.14 us (1%)
    all_gather x1, waiting for transfers between devices, shards(): lax.all_gather(stacked, 'seq', axis=2, tiled=True)  93.4 us
    reduce_scatter x1, waiting for transfers between devices, shards(): lax.psum_scatter(partial_terms.astype(jnp.bfloat16), 'head', scatter_dime...  41.9 us
    pallas_call x1, Pallas kernels, update_centroids(): pl.pallas_call(body, name='centroids', out_shape=(jax.ShapeDtypeStruct((r...  38.7 us
    dot_general x1, matrix products, shards(): jnp.einsum('td,dkc->tkc', hidden_states, lax.all_gather(stacked, 'seq', a...  7.37 us
  transfers between devices with their start and end apart: 2, of which 2 were waited for; matrix products, arithmetic and copies ran while one was open for 1% of the time, Pallas kernels for 0%

profile of v1, /device:TPU:1, one launch (start us, length us, event | category | flops | bytes accessed | tf_op | source)
XLA Modules:
  0.0 210.1 jit_solution(15437743511841647534)
XLA Ops:
  7.2 0.0 copy-start
  7.2 0.0 all-gather.2.cloned.1.call-start
  7.2 1.5 pad_maximum_fusion
  8.7 0.0 all-gather.2.cloned.1.call-update
  8.8 0.0 reduce-scatter.2.cloned.1.call-start
  8.8 93.4 %all-gather.2.cloned.1.call-done = bf16[1024,2,1024]{0,2,1:T(8,128)(2,1)} async-done(((bf16[1024,2,16]{0,2,1:T(8,128)(2,1)}), bf16[1024,2,1024]{0,2,1:T(8,128)(2,1)}) %all-gather.2.cloned.1.call-update) | async-done | bytes 4194320 | tf_op jit(solution)/shard_map/all_gather | solution.py:107
  102.3 0.0 copy-done
  102.3 7.4 %convert_bitcast_fusion = bf16[768,2,1024]{0,2,1:T(8,128)(2,1)} fusion(bf16[1024,2,1024]{0,2,1:T(8,128)(2,1)} %all-gather.2.cloned.1.call-done, bf16[768,1024]{1,0:T(8,128)(2,1)S(1)} %copy-done), kind=kOutput, calls=%fused_computation.3 | convolution fusion | flops 3222798336 | bytes 8912896 | tf_op jit(solution)/shard_map/td,dkc->tkc/dot_general | solution.py:104
  109.6 0.0 copy-start.3
  109.6 0.0 reduce-scatter.2.cloned.1.call-update
  109.7 0.7 copy-done.3
  110.3 0.4 convert_reduce_fusion
  110.7 0.1 reshape.43
  110.8 0.6 pad.4.refs_1_
  111.4 1.3 dynamic-slice_bitcast_fusion.refs_2_
  112.7 41.9 %reduce-scatter.2.cloned.1.call-done = bf16[768,2,128]{0,2,1:T(8,128)(2,1)} async-done(((bf16[768,2,1024]{0,2,1:T(8,128)(2,1)}), bf16[768,2,128]{0,2,1:T(8,128)(2,1)}) %reduce-scatter.2.cloned.1.call-update) | async-done | bytes 393232 | tf_op jit(solution)/shard_map/reduce_scatter | solution.py:110
  154.6 0.0 copy-start.1
  154.6 1.1 slice_bitcast_fusion
  155.7 0.8 copy.18
  156.5 0.8 copy.19
  157.3 2.4 %fusion.refs_0_ = f32[64,16,128]{2,1,0:T(8,128)} fusion(s32[64,16]{1,0:T(8,128)S(1)} %multiply_add_fusion, s32[768]{0:T(1024)S(1)} %reduce.1, bf16[768,2,128]{0,2,1:T(8,128)(2,1)} %reduce-scatter.2.cloned.1.call-done), kind=kOutput, calls=%fused_computation.4 | convolution fusion | flops 202113024 | bytes 728064 | tf_op jit(solution)/shard_map/tc,te->ce/dot_general | solution.py:116
  159.7 38.7 %centroids.1 = (f32[16,128]{1,0:T(8,128)}, bf16[64,16,128]{2,1,0:T(8,128)(2,1)}) custom-call(f32[64,16,128]{2,1,0:T(8,128)} %fusion.refs_0_, f32[64,1,128]{2,1,0:T(1,128)} %pad.4.refs_1_, f32[16,128]{1,0:T(8,128)} %dynamic-slice_bitcast_fusion.refs_2_), custom_call_target="tpu_custom_call" | custom-call | tf_op jit(solution)/shard_map/centroids/pallas_call | solution.py:78
  198.4 0.0 copy-start.2
  198.4 1.2 multiply_reduce_fusion
  199.6 0.1 add.22
  199.7 0.0 copy-done.1
  199.7 0.1 multiply_reduce_fusion.1
  199.7 2.9 %fusion.5 = bf16[1,768,1024]{2,1,0:T(8,128)(2,1)} fusion(f32[1024]{0:T(1024)S(1)} %add.22, bf16[1024,128]{1,0:T(8,128)(2,1)} %bitcast.27, f32[768]{0:T(1024)S(1)} %multiply_reduce_fusion.1, bf16[768,2,128]{0,2,1:T(8,128)(2,1)S(1)} %copy-done.1), kind=kOutput, calls=%fused_computation.9 | convolution fusion | flops 205258752 | bytes 2039808 | tf_op jit(solution)/shard_map/te,ce->tc/dot_general | solution.py:132
  202.6 0.0 copy-done.2
  202.6 0.6 copy.23
  (2 shorter events, 0.0 us)
Async XLA Ops:
  7.2 95.1 %copy-start = (bf16[768,1024]{1,0:T(8,128)(2,1)S(1)}, bf16[768,1024]{1,0:T(8,128)(2,1)}, u32[]{:S(2)}) copy-start(bf16[768,1024]{1,0:T(8,128)(2,1)} %param.5) | copy-start | bytes 4718596
  7.2 95.1 %all-gather.2.cloned.1.call-start = ((), (), s32[]{:S(2)}) async-start(), calls=%async_computation.1 | async-start | bytes 4259840 | tf_op jit(solution)/shard_map/all_gather | solution.py:107
  8.8 145.8 %reduce-scatter.2.cloned.1.call-start = ((), (), s32[]{:S(2)}) async-start(), calls=%async_computation.2 | async-start | bytes 3538944 | tf_op jit(solution)/shard_map/reduce_scatter | solution.py:110
  109.6 0.7 copy-start.3
  154.6 45.1 %copy-start.1 = (bf16[768,2,128]{0,2,1:T(8,128)(2,1)S(1)}, bf16[768,2,128]{0,2,1:T(8,128)(2,1)}, u32[]{:S(2)}) copy-start(bf16[768,2,128]{0,2,1:T(8,128)(2,1)} %reduce-scatter.2.cloned.1.call-done) | copy-start | bytes 1179652
  198.4 4.2 %copy-start.2 = (f32[16,128]{1,0:T(8,128)S(1)}, f32[16,128]{1,0:T(8,128)}, u32[]{:S(2)}) copy-start(f32[16,128]{1,0:T(8,128)} %get-tuple-element.6) | copy-start | bytes 24580
Sparse Core Ops, SparseCore 0:
  12.0 90.2 all-gather.1
  109.8 44.7 reduce-scatter.1

commit v2 on v1

--- a/solution.py
+++ b/solution.py
@@ -6,6 +6,8 @@
 from jax.sharding import PartitionSpec as P
 
 MESH = pl.DeviceIdType.MESH
+NX, NY, NZ = 4, 8, 8
+PIECES = 2
 
 
 def centroid_kernel(
@@ -95,23 +97,183 @@
     )(sums, counts, old_own)
 
 
+def project_kernel(h_ref, w_ref, k_ref, v_ref, held, part, plus, minus, send, recv, zsend, zrecv):
+    me = lax.axis_index("seq")
+    z = lax.axis_index("head")
+    core = lax.rem(me, 2)
+    x = lax.rem(me // 2, NX)
+    y = me // (2 * NX)
+
+    def at(y_, x_, core_):
+        return {"seq": (lax.rem(y_, NY) * NX + lax.rem(x_, NX)) * 2 + core_}
+
+    above, below = at(y + 1, x, core), at(y + NY - 1, x, core)
+    partner = at(y, x, 1 - core)
+    z_up, z_down = {"head": lax.rem(z + 1, NZ)}, {"head": lax.rem(z + NZ - 1, NZ)}
+    x_peers = [at(y, x + NX - k, core) for k in range(1, NX)]
+
+    barrier = pltpu.get_barrier_semaphore()
+    peers = [above, below, partner, z_up, z_down] + x_peers
+    for peer in peers:
+        pl.semaphore_signal(barrier, inc=1, device_id=peer, device_id_type=MESH)
+    pl.semaphore_wait(barrier, len(peers))
+
+    sent = []
+
+    def block(row, k, c=core):
+        return held.at[lax.rem(row, NY), c, lax.rem(x + k, NX)]
+
+    def copy(ref, i, to):
+        return pltpu.make_async_remote_copy(
+            src_ref=ref, dst_ref=ref, send_sem=send.at[i], recv_sem=recv.at[i],
+            device_id=to, device_id_type=MESH,
+        )
+
+    def push(ref, i, to):
+        c = copy(ref, i, to)
+        c.start()
+        sent.append(c)
+
+    def up(s, k):
+        return (s - 1) * NX + k
+
+    def down(s, k):
+        return 16 + (s - 1) * NX + k
+
+    def side(i):
+        return 36 + i
+
+    own = pltpu.make_async_copy(w_ref, block(y, 0), send.at[72])
+    own.start()
+    own.wait()
+    for k in range(1, NX):
+        ref = block(y, 0)
+        push(ref, 68 + k, x_peers[k - 1])
+    for k in range(NX):
+        ref = block(y, k)
+        if k:
+            copy(ref, 68 + k, partner).wait_recv()
+        push(ref, up(1, k), above)
+        push(ref, down(1, k), below)
+        push(ref, 32 + k, partner)
+
+    def project(row):
+        head = lax.rem(row, NY)
+        weights = jnp.concatenate(
+            [held[head, c, i, j] for j in range(2) for i in range(NX) for c in range(2)], axis=0
+        )
+
+        def rows(i, carry):
+            at_rows = pl.ds(pl.multiple_of(i * 256, 256), 256)
+            out = lax.dot_general(
+                h_ref[at_rows, :], weights, (((1,), (1,)), ((), ())),
+                preferred_element_type=jnp.float32,
+            ).astype(jnp.bfloat16)
+            part[head, 0, at_rows, :] = out[:, :128]
+            part[head, 1, at_rows, :] = out[:, 128:]
+            return carry
+
+        lax.fori_loop(0, h_ref.shape[0] // 256, rows, 0)
+
+    for k in range(NX):
+        copy(block(y, k, 1 - core), 32 + k, partner).wait_recv()
+    project(y)
+    half = NY // 2
+    for s in range(1, half + 1):
+        ups = [k for k in range(NX) if s < half or k < NX // 2]
+        downs = [k for k in range(NX) if s < half or k >= NX // 2]
+        for k in range(NX):
+            if k in ups:
+                ref = block(y + NY - s, k)
+                copy(ref, up(s, k), partner).wait_recv()
+                if s < half - 1 or (s == half - 1 and k < NX // 2):
+                    push(ref, up(s + 1, k), above)
+                push(ref, side(up(s, k)), partner)
+            if k in downs:
+                ref = block(y + s, k)
+                copy(ref, down(s, k), partner).wait_recv()
+                if s < half - 1 or (s == half - 1 and k >= NX // 2):
+                    push(ref, down(s + 1, k), below)
+                push(ref, side(down(s, k)), partner)
+        for k in ups:
+            copy(block(y + NY - s, k, 1 - core), side(up(s, k)), partner).wait_recv()
+        if s < half:
+            project(y + NY - s)
+        for k in downs:
+            copy(block(y + s, k, 1 - core), side(down(s, k)), partner).wait_recv()
+        project(y + s)
+
+    tall = h_ref.shape[0] // PIECES
+
+    def ring(src, dst, i, to):
+        c = pltpu.make_async_remote_copy(
+            src_ref=src, dst_ref=dst, send_sem=zsend.at[i], recv_sem=zrecv.at[i],
+            device_id=to, device_id_type=MESH,
+        )
+        return c
+
+    def ring_push(src, dst, i, to):
+        c = ring(src, dst, i, to)
+        c.start()
+        sent.append(c)
+
+    ways = ((0, plus, z_up, NZ - 1, k_ref), (1, minus, z_down, 1, v_ref))
+    for p in range(PIECES):
+        rows = pl.ds(p * tall, tall)
+        for j, slots, to, step, _ in ways:
+            src = part.at[lax.rem(z + step, NZ), j, rows]
+            ring_push(src, slots.at[0, rows], (j * (NZ - 1)) * PIECES + p, to)
+    for s in range(NZ - 1):
+        for p in range(PIECES):
+            rows = pl.ds(p * tall, tall)
+            for j, slots, to, step, out in ways:
+                i = (j * (NZ - 1) + s) * PIECES + p
+                here = slots.at[s, rows]
+                ring(here, here, i, to).wait_recv()
+                head = lax.rem(z + step * (s + 2), NZ)
+                total = slots[s, rows].astype(jnp.float32) + part[head, j, rows].astype(jnp.float32)
+                total = total.astype(jnp.bfloat16)
+                if s < NZ - 2:
+                    slots[s, rows] = total
+                    ring_push(here, slots.at[s + 1, rows], i + PIECES, to)
+                else:
+                    out[rows, :] = total
+    for c in sent:
+        c.wait_send()
+
+
+def project_keys(hidden, weights):
+    tok_rows = hidden.shape[0]
+    vmem = pl.BlockSpec(memory_space=pltpu.VMEM)
+    out = jax.ShapeDtypeStruct((tok_rows, 128), jnp.bfloat16)
+    n_ring = 2 * (NZ - 1) * PIECES
+    return pl.pallas_call(
+        project_kernel,
+        name="project",
+        out_shape=(out, out),
+        in_specs=[vmem] * 2,
+        out_specs=(vmem, vmem),
+        scratch_shapes=[
+            pltpu.VMEM((NY, 2, NX) + weights.shape, jnp.bfloat16),
+            pltpu.VMEM((NZ, 2, tok_rows, 128), jnp.bfloat16),
+            pltpu.VMEM((NZ - 1, tok_rows, 128), jnp.bfloat16),
+            pltpu.VMEM((NZ - 1, tok_rows, 128), jnp.bfloat16),
+            pltpu.SemaphoreType.DMA((73,)),
+            pltpu.SemaphoreType.DMA((73,)),
+            pltpu.SemaphoreType.DMA((n_ring,)),
+            pltpu.SemaphoreType.DMA((n_ring,)),
+        ],
+        compiler_params=pltpu.CompilerParams(collective_id=1, has_side_effects=True),
+    )(hidden, weights)
+
+
 def shards(hidden_states, k_weight, v_weight, assignments, old_centroids):
     tok_rows = hidden_states.shape[0]
     clusters = old_centroids.shape[1]
     head_size = old_centroids.shape[2]
     n_seq = lax.axis_size("seq")
-    stacked = jnp.stack((k_weight, v_weight), axis=1)
-    partial_terms = jnp.einsum(
-        "td,dkc->tkc",
-        hidden_states,
-        lax.all_gather(stacked, "seq", axis=2, tiled=True),
-        preferred_element_type=jnp.float32,
-    )
-    summed = lax.psum_scatter(
-        partial_terms.astype(jnp.bfloat16), "head", scatter_dimension=2, tiled=True
-    ).astype(jnp.float32)
-    keys = summed[:, 0].astype(jnp.bfloat16)
-    value_cache = summed[:, 1].astype(jnp.bfloat16)
+    weights = jnp.stack((k_weight.T, v_weight.T), axis=0)
+    keys, value_cache = project_keys(hidden_states, weights)
     onehot = assignments[0][:, None] == jnp.arange(clusters, dtype=jnp.int32)[None, :]
     local_sums = jnp.einsum(
         "tc,te->ce", onehot.astype(jnp.bfloat16), keys, preferred_element_type=jnp.float32

time: 210 us -> 124 us (0.59)
  waiting for transfers between devices: 135 us -> 0 us
  Pallas kernels: 38.7 us -> 110 us
  between operations: 14.1 us -> 0.73 us
  matrix products: 12.6 us -> 5.66 us
    all_gather x1 -> x0, waiting for transfers between devices: 93.4 us -> none  [shards(): lax.all_gather(stacked, 'seq', axis=2, tiled=True)]
    pallas_call x0 -> x1, Pallas kernels: none -> 74.8 us  [project_keys(): pl.pallas_call(project_kernel, name='project', out_shape=(out, out), in_s...]
    reduce_scatter x1 -> x0, waiting for transfers between devices: 41.9 us -> none  [shards(): lax.psum_scatter(partial_terms.astype(jnp.bfloat16), 'head', scatter_dime...]
    dot_general x1 -> x0, matrix products: 7.37 us -> none  [shards(): jnp.einsum('td,dkc->tkc', hidden_states, lax.all_gather(stacked, 'seq', a...]
    pallas_call x1, Pallas kernels: 38.7 us -> 35.2 us  [update_centroids(): pl.pallas_call(body, name='centroids', out_shape=(jax.ShapeDtypeStruct((r...]
  transfers between devices with their start and end apart: 2 -> 0, of which waited for: 2 -> 0; matrix products, arithmetic and copies ran while one was open for 1% -> 0% of each run, Pallas kernels for 0% -> 0%
where the time goes in v2:
time: 124 us
  Pallas kernels  110 us (89%)
  matrix products  5.66 us (5%)
  local copies, waits for them, and re-layouts  4.39 us (4%)
  other arithmetic  3.14 us (3%)
    pallas_call x1, Pallas kernels, project_keys(): pl.pallas_call(project_kernel, name='project', out_shape=(out, out), in_s...  74.8 us
    pallas_call x1, Pallas kernels, update_centroids(): pl.pallas_call(body, name='centroids', out_shape=(jax.ShapeDtypeStruct((r...  35.2 us
    unnamed x13, local copies, waits for them, and re-layouts  2.99 us
    dot_general x1, matrix products, shards(): jnp.einsum('tc,te->ce', onehot.astype(jnp.bfloat16), keys, preferred_elem...  2.89 us
    dot_general x1, matrix products, shards(): jnp.einsum('te,ce->tc', keys, low, preferred_element_type=jnp.float32)  2.77 us

profile of v2, /device:TPU:1, one launch (start us, length us, event | category | flops | bytes accessed | tf_op | source)
XLA Modules:
  0.0 123.9 jit_solution(3669747034611633179)
XLA Ops:
  0.6 0.0 copy-start
  0.6 0.0 copy-start.4
  0.7 1.0 copy-done
  1.7 0.6 dynamic-slice_bitcast_fusion.refs_2_
  2.3 1.4 %pad_maximum_fusion.w_ref = bf16[2,16,1024]{2,1,0:T(8,128)(2,1)} fusion(bf16[1,16,1024]{2,1,0:T(8,128)(2,1)} %bitcast.20, bf16[1,16,1024]{2,1,0:T(8,128)(2,1)} %bitcast.21), kind=kLoop, calls=%fused_computation.8 | loop fusion | flops 32768 | bytes 131072 | tf_op jit(solution)/shard_map/stack | solution.py:275
  3.7 74.8 %project.1 = (bf16[768,128]{1,0:T(8,128)(2,1)}, bf16[768,128]{1,0:T(8,128)(2,1)}) custom-call(bf16[768,1024]{1,0:T(8,128)(2,1)} %h_ref.1, bf16[2,16,1024]{2,1,0:T(8,128)(2,1)} %pad_maximum_fusion.w_ref), custom_call_target="tpu_custom_call" | custom-call | tf_op jit(solution)/shard_map/project/pallas_call | solution.py:250
  78.5 0.0 copy-start.1
  78.5 0.0 copy-done.4
  78.6 2.9 %fusion = f32[1024,128]{1,0:T(8,128)} fusion(bf16[768,128]{1,0:T(8,128)(2,1)} %get-tuple-element.16, s32[768]{0:T(1024)S(1)} %reduce.1), kind=kOutput, calls=%fused_computation.3 | convolution fusion | flops 202113024 | bytes 723968 | tf_op jit(solution)/shard_map/tc,te->ce/dot_general | solution.py:278
  81.5 0.4 convert_reduce_fusion
  81.8 0.1 reshape.24
  81.9 0.6 pad.4.refs_1_
  82.6 35.2 %centroids.1 = (f32[16,128]{1,0:T(8,128)}, bf16[64,16,128]{2,1,0:T(8,128)(2,1)}) custom-call(f32[64,16,128]{2,1,0:T(8,128)} %bitcast.17, f32[64,1,128]{2,1,0:T(1,128)} %pad.4.refs_1_, f32[16,128]{1,0:T(8,128)} %dynamic-slice_bitcast_fusion.refs_2_), custom_call_target="tpu_custom_call" | custom-call | tf_op jit(solution)/shard_map/centroids/pallas_call | solution.py:80
  117.7 1.2 multiply_reduce_fusion
  118.9 0.1 add.16
  119.0 0.0 copy-done.1
  119.0 0.2 multiply_reduce_fusion.1
  119.2 0.0 copy-start.2
  119.2 0.0 copy-start.3
  119.2 2.8 %fusion.2 = bf16[1,768,1024]{2,1,0:T(8,128)(2,1)} fusion(f32[1024]{0:T(1024)S(1)} %add.16, bf16[768,128]{1,0:T(8,128)(2,1)S(1)} %copy-done.1, bf16[1024,128]{1,0:T(8,128)(2,1)} %bitcast.18, f32[768]{0:T(1024)S(1)} %multiply_reduce_fusion.1), kind=kOutput, calls=%fused_computation.5 | convolution fusion | flops 205258752 | bytes 2038784 | tf_op jit(solution)/shard_map/te,ce->tc/dot_general | solution.py:294
  122.0 0.7 copy.14
  122.6 0.0 copy-done.2
  122.6 0.7 copy.15
  123.3 0.0 copy-done.3
  123.3 0.6 copy.16
  (1 shorter events, 0.0 us)
Async XLA Ops:
  0.6 1.0 copy-start
  0.6 77.9 %copy-start.4 = (s32[1,768]{1,0:T(1,128)S(1)}, s32[1,768]{1,0:T(1,128)}, u32[]{:S(2)}) copy-start(s32[1,768]{1,0:T(1,128)} %param.8) | copy-start | bytes 9220
  78.5 40.5 %copy-start.1 = (bf16[768,128]{1,0:T(8,128)(2,1)S(1)}, bf16[768,128]{1,0:T(8,128)(2,1)}, u32[]{:S(2)}) copy-start(bf16[768,128]{1,0:T(8,128)(2,1)} %get-tuple-element.16) | copy-start | bytes 589828
  119.2 3.5 %copy-start.2 = (bf16[768,128]{1,0:T(8,128)(2,1)S(1)}, bf16[768,128]{1,0:T(8,128)(2,1)}, u32[]{:S(2)}) copy-start(bf16[768,128]{1,0:T(8,128)(2,1)} %get-tuple-element.17) | copy-start | bytes 589828
  119.2 4.1 %copy-start.3 = (f32[16,128]{1,0:T(8,128)S(1)}, f32[16,128]{1,0:T(8,128)}, u32[]{:S(2)}) copy-start(f32[16,128]{1,0:T(8,128)} %get-tuple-element.10) | copy-start | bytes 24580

commit v3 on v1

v3 whole, which is shorter than its diff:
```python
import jax
import jax.numpy as jnp
from jax import lax
from jax.experimental import pallas as pl
from jax.experimental.pallas import tpu as pltpu
from jax.sharding import PartitionSpec as P

MESH = pl.DeviceIdType.MESH
NX, NY, NZ = 4, 8, 8
CHIPS = NX * NY
PIECES = 2


def remote(src, dst, send_sem, recv_sem, to):
    return pltpu.make_async_remote_copy(
        src_ref=src, dst_ref=dst, send_sem=send_sem, recv_sem=recv_sem,
        device_id=to, device_id_type=MESH,
    )


def z_neighbours():
    z = lax.axis_index("head")
    return {"head": lax.rem(z + 1, NZ)}, {"head": lax.rem(z + NZ - 1, NZ)}


class Ring:
    def __init__(self, part, out, plus, minus, send, recv, sent):
        self.part, self.out, self.send, self.recv, self.sent = part, out, send, recv, sent
        self.z = lax.axis_index("head")
        up, down = z_neighbours()
        self.half = out.shape[0] // 2
        self.tall = self.half // PIECES
        self.ways = ((0, plus, up, NZ - 1), (1, minus, down, 1))

    def copy(self, src, dst, i, to):
        return remote(src, dst, self.send.at[i], self.recv.at[i], to)

    def push(self, src, dst, i, to):
        c = self.copy(src, dst, i, to)
        c.start()
        self.sent.append(c)

    def start(self):
        for p in range(PIECES):
            for j, slots, to, step in self.ways:
                src = self.part.at[
                    lax.rem(self.z + step, NZ), pl.ds(j * self.half + p * self.tall, self.tall)
                ]
                dst = slots.at[0, pl.ds(p * self.tall, self.tall)]
                self.push(src, dst, j * (NZ - 1) * PIECES + p, to)

    def step(self, s):
        for p in range(PIECES):
            rows = pl.ds(p * self.tall, self.tall)
            for j, slots, to, step in self.ways:
                i = (j * (NZ - 1) + s) * PIECES + p
                here = slots.at[s, rows]
                full = pl.ds(j * self.half + p * self.tall, self.tall)
                self.copy(here, here, i, to).wait_recv()
                head = lax.rem(self.z + step * (s + 2), NZ)
                total = slots[s, rows].astype(jnp.float32) + self.part[head, full].astype(jnp.float32)
                total = total.astype(jnp.bfloat16)
                if s < NZ - 2:
                    slots[s, rows] = total
                    self.push(here, slots.at[s + 1, rows], i + PIECES, to)
                else:
                    self.out[full, :] = total


def ring_scratch(tok_rows):
    n_ring = 2 * (NZ - 1) * PIECES
    return [
        pltpu.VMEM((NZ - 1, tok_rows // 2, 128), jnp.bfloat16),
        pltpu.VMEM((NZ - 1, tok_rows // 2, 128), jnp.bfloat16),
        pltpu.SemaphoreType.DMA((n_ring,)),
        pltpu.SemaphoreType.DMA((n_ring,)),
    ]


def enter(peers, chips=None):
    barrier = pltpu.get_barrier_semaphore()
    for peer in peers:
        pl.semaphore_signal(barrier, inc=1, device_id=peer, device_id_type=MESH)
    count = len(peers)
    if chips is not None:

        def greet(d, c):
            pl.semaphore_signal(barrier, inc=1, device_id=chips(d), device_id_type=MESH)
            return c

        lax.fori_loop(1, CHIPS, greet, 0)
        count += CHIPS - 1
    pl.semaphore_wait(barrier, count)


def project_kernel(
    h_ref, w_ref, k_ref, pv_ref, held, pk, send, recv, own_sem, plus, minus, zsend, zrecv
):
    me = lax.axis_index("seq")
    core = lax.rem(me, 2)
    x = lax.rem(me // 2, NX)
    y = me // (2 * NX)

    def at(y_, x_, core_):
        return {"seq": (lax.rem(y_, NY) * NX + lax.rem(x_, NX)) * 2 + core_}

    above, below = at(y + 1, x, core), at(y + NY - 1, x, core)
    partner = at(y, x, 1 - core)
    z_up, z_down = z_neighbours()
    x_peers = [at(y, x + NX - k, core) for k in range(1, NX)]
    enter([above, below, partner, z_up, z_down] + x_peers)

    sent = []
    parts = (pk, pv_ref)

    def block(j, row, k, c=core):
        return held.at[j, lax.rem(row, NY), c, lax.rem(x + k, NX)]

    def copy(j, ref, i, to):
        return remote(ref, ref, send.at[j, i], recv.at[j, i], to)

    def push(j, ref, i, to):
        c = copy(j, ref, i, to)
        c.start()
        sent.append(c)

    def up(s, k):
        return (s - 1) * NX + k

    def down(s, k):
        return 16 + (s - 1) * NX + k

    def side(i):
        return 36 + i

    def project(j, rows_y):
        heads = [lax.rem(row, NY) for row in rows_y]
        weights = jnp.concatenate(
            [held[j, head, c, i] for head in heads for i in range(NX) for c in range(2)], axis=0
        )

        def rows(i, carry):
            at_rows = pl.ds(pl.multiple_of(i * 256, 256), 256)
            out = lax.dot_general(
                h_ref[at_rows, :], weights, (((1,), (1,)), ((), ())),
                preferred_element_type=jnp.float32,
            ).astype(jnp.bfloat16)
            for q, head in enumerate(heads):
                parts[j][head, at_rows, :] = out[:, q * 128:(q + 1) * 128]
            return carry

        lax.fori_loop(0, h_ref.shape[0] // 256, rows, 0)

    def first(j):
        for k in range(NX):
            ref = block(j, y, k)
            if k:
                copy(j, ref, 68 + k, partner).wait_recv()
            push(j, ref, up(1, k), above)
            push(j, ref, down(1, k), below)
            push(j, ref, 32 + k, partner)

    def mine(j):
        for k in range(NX):
            copy(j, block(j, y, k, 1 - core), 32 + k, partner).wait_recv()
        project(j, [y])

    half = NY // 2

    def relay(j, s):
        ups = [k for k in range(NX) if s < half or k < NX // 2]
        downs = [k for k in range(NX) if s < half or k >= NX // 2]
        for k in range(NX):
            if k in ups:
                ref = block(j, y + NY - s, k)
                copy(j, ref, up(s, k), partner).wait_recv()
                if s < half - 1 or (s == half - 1 and k < NX // 2):
                    push(j, ref, up(s + 1, k), above)
                push(j, ref, side(up(s, k)), partner)
            if k in downs:
                ref = block(j, y + s, k)
                copy(j, ref, down(s, k), partner).wait_recv()
                if s < half - 1 or (s == half - 1 and k >= NX // 2):
                    push(j, ref, down(s + 1, k), below)
                push(j, ref, side(down(s, k)), partner)
        for k in ups:
            copy(j, block(j, y + NY - s, k, 1 - core), side(up(s, k)), partner).wait_recv()
        for k in downs:
            copy(j, block(j, y + s, k, 1 - core), side(down(s, k)), partner).wait_recv()
        project(j, [y + NY - s, y + s] if s < half else [y + s])

    own = [
        pltpu.make_async_copy(w_ref.at[j], block(j, y, 0), own_sem.at[j]) for j in range(2)
    ]
    for j in range(2):
        own[j].start()
    for j in range(2):
        own[j].wait()
        for k in range(1, NX):
            push(j, block(j, y, 0), 68 + k, x_peers[k - 1])
    first(0)
    mine(0)
    for s in range(1, half + 1):
        relay(0, s)
    ring = Ring(pk, k_ref, plus, minus, zsend, zrecv, sent)
    ring.start()
    first(1)
    mine(1)
    for s in range(NZ - 1):
        ring.step(s)
        if s in (0, 2, 4, 5):
            relay(1, (0, 2, 4, 5).index(s) + 1)
    for c in sent:
        c.wait_send()


def project_keys(hidden, weights):
    tok_rows = hidden.shape[0]
    vmem = pl.BlockSpec(memory_space=pltpu.VMEM)
    return pl.pallas_call(
        project_kernel,
        name="project",
        out_shape=(
            jax.ShapeDtypeStruct((tok_rows, 128), jnp.bfloat16),
            jax.ShapeDtypeStruct((NZ, tok_rows, 128), jnp.bfloat16),
        ),
        in_specs=[vmem] * 2,
        out_specs=(vmem, vmem),
        scratch_shapes=[
            pltpu.VMEM((2, NY, 2, NX) + weights.shape[1:], jnp.bfloat16),
            pltpu.VMEM((NZ, tok_rows, 128), jnp.bfloat16),
            pltpu.SemaphoreType.DMA((2, 72)),
            pltpu.SemaphoreType.DMA((2, 72)),
            pltpu.SemaphoreType.DMA((2,)),
        ] + ring_scratch(tok_rows),
        compiler_params=pltpu.CompilerParams(collective_id=1, has_side_effects=True),
    )(hidden, weights)


def centroid_kernel(
    prior, sums_ref, cnt_ref, old_ref, pv_ref, new_ref, low_ref, v_ref,
    pair, pair_cnt, mix, mix_cnt, got, got_cnt, low, send, recv, plus, minus, zsend, zrecv
):
    me = lax.axis_index("seq")
    core = lax.rem(me, 2)
    chip = me // 2
    partner = {"seq": chip * 2 + 1 - core}
    z_up, z_down = z_neighbours()

    def peer(d):
        return {"seq": lax.rem(chip + d, CHIPS) * 2 + core}

    enter([partner, z_up, z_down], peer)

    def copy(src, dst, k, to):
        return remote(src, dst, send.at[k], recv.at[k], to)

    sent = []
    ring = Ring(pv_ref, v_ref, plus, minus, zsend, zrecv, sent)
    to_pair = copy(sums_ref.at[:, 1 - core], pair, 0, partner)
    to_pair_cnt = copy(cnt_ref.at[:, 1 - core], pair_cnt, 1, partner)
    to_pair.start()
    to_pair_cnt.start()
    ring.start()
    to_pair.wait_recv()
    to_pair_cnt.wait_recv()

    def merge(i, c):
        mix[i] = sums_ref[i, core] + pair[i]
        mix_cnt[i] = cnt_ref[i, core] + pair_cnt[i]
        return c

    lax.fori_loop(0, CHIPS, merge, 0)

    def scatter(d, c):
        to = lax.rem(chip + d, CHIPS)
        copy(mix.at[to], got.at[d - 1], 2, peer(d)).start()
        copy(mix_cnt.at[to], got_cnt.at[d - 1], 3, peer(d)).start()
        return c

    lax.fori_loop(1, CHIPS, scatter, 0)
    for s in range(3):
        ring.step(s)
    copy(got, got, 2, partner).wait_recv()
    copy(got_cnt, got_cnt, 3, partner).wait_recv()

    def add(i, c):
        return c[0] + got[i], c[1] + got_cnt[i]

    total, cnt = lax.fori_loop(0, CHIPS - 1, add, (mix[chip], mix_cnt[chip]))
    rows = total.shape[0]
    lane = lax.broadcasted_iota(jnp.int32, (rows, 128), 1)
    row = lax.broadcasted_iota(jnp.int32, (rows, 128), 0)
    count = jnp.sum(
        jnp.where(lane == row, jnp.broadcast_to(cnt, (rows, 128)), 0.0), axis=1, keepdims=True
    )
    new = (total + prior * old_ref[...]) / (count + prior)
    new_ref[...] = new
    low[core, chip] = new.astype(jnp.bfloat16)

    def gather(d, c):
        copy(low.at[core, chip], low.at[core, chip], 4, peer(d)).start()
        return c

    lax.fori_loop(1, CHIPS, gather, 0)
    for s in range(3, 6):
        ring.step(s)
    rest = low.at[core, pl.ds(0, CHIPS - 1)]
    copy(rest, rest, 4, partner).wait_recv()
    back = copy(low.at[core], low.at[core], 5, partner)
    back.start()
    ring.step(6)
    back.wait_recv()
    low_ref[:, 0] = low[0]
    low_ref[:, 1] = low[1]
    to_pair.wait_send()
    to_pair_cnt.wait_send()
    copy(got, got, 2, partner).wait_send()
    copy(got_cnt, got_cnt, 3, partner).wait_send()
    copy(rest, rest, 4, partner).wait_send()
    back.wait_send()
    for c in sent:
        c.wait_send()


def update_centroids(sums, counts, old_own, part_v, prior):
    rows, width = old_own.shape
    tok_rows = part_v.shape[1]
    vmem = pl.BlockSpec(memory_space=pltpu.VMEM)

    def body(*refs):
        centroid_kernel(prior, *refs)

    return pl.pallas_call(
        body,
        name="centroids",
        out_shape=(
            jax.ShapeDtypeStruct((rows, width), jnp.float32),
            jax.ShapeDtypeStruct((CHIPS, 2, rows, width), jnp.bfloat16),
            jax.ShapeDtypeStruct((tok_rows, 128), jnp.bfloat16),
        ),
        in_specs=[vmem] * 4,
        out_specs=(vmem, vmem, vmem),
        scratch_shapes=[
            pltpu.VMEM((CHIPS, rows, width), jnp.float32),
            pltpu.VMEM((CHIPS, 1, 128), jnp.float32),
            pltpu.VMEM((CHIPS, rows, width), jnp.float32),
            pltpu.VMEM((CHIPS, 1, 128), jnp.float32),
            pltpu.VMEM((CHIPS - 1, rows, width), jnp.float32),
            pltpu.VMEM((CHIPS - 1, 1, 128), jnp.float32),
            pltpu.VMEM((2, CHIPS, rows, width), jnp.bfloat16),
            pltpu.SemaphoreType.DMA((6,)),
            pltpu.SemaphoreType.DMA((6,)),
        ] + ring_scratch(tok_rows),
        compiler_params=pltpu.CompilerParams(collective_id=0, has_side_effects=True),
    )(sums, counts, old_own, part_v)


def shards(hidden_states, k_weight, v_weight, assignments, old_centroids):
    tok_rows = hidden_states.shape[0]
    clusters = old_centroids.shape[1]
    head_size = old_centroids.shape[2]
    n_seq = lax.axis_size("seq")
    weights = jnp.stack((k_weight.T, v_weight.T), axis=0)
    keys, part_v = project_keys(hidden_states, weights)
    onehot = assignments[0][:, None] == jnp.arange(clusters, dtype=jnp.int32)[None, :]
    local_sums = jnp.einsum(
        "tc,te->ce", onehot.astype(jnp.bfloat16), keys, preferred_element_type=jnp.float32
    )
    local_counts = jnp.sum(onehot.astype(jnp.float32), axis=0)
    prior_weight = float(tok_rows * n_seq // clusters)
    share = clusters // n_seq
    counts = jnp.pad(
        local_counts.reshape(CHIPS, 2, 1, share), ((0, 0), (0, 0), (0, 0), (0, 128 - share))
    )
    old_own = lax.dynamic_slice_in_dim(old_centroids[0], lax.axis_index("seq") * share, share, 0)
    new_own, low, value_cache = update_centroids(
        local_sums.reshape(CHIPS, 2, share, head_size), counts, old_own, part_v, prior_weight
    )
    low = low.reshape(clusters, head_size)
    wide = low.astype(jnp.float32)
    centroid_square = jnp.sum(wide * wide, axis=1)
    key_wide = keys.astype(jnp.float32)
    key_square = jnp.sum(key_wide * key_wide, axis=1)
    cross_term = jnp.einsum("te,ce->tc", keys, low, preferred_element_type=jnp.float32)
    dist = (key_square[:, None] - 2.0 * cross_term + centroid_square[None, :]) / head_size
    return (keys, value_cache, new_own[None], dist.astype(jnp.bfloat16)[None])


def solution(mesh):
    in_specs = (
        P("seq", "head"),
        P("head", "seq"),
        P("head", "seq"),
        P("head", "seq"),
        P("head", None, None),
    )
    out_specs = (P("seq", "head"), P("seq", "head"), P("head", "seq", None), P("head", "seq", None))
    return jax.shard_map(shards, mesh=mesh, in_specs=in_specs, out_specs=out_specs, check_vma=False)
```

time: 210 us -> 113 us (0.54)
  waiting for transfers between devices: 135 us -> 0 us
  Pallas kernels: 38.7 us -> 98.1 us
  between operations: 14.1 us -> 0.73 us
  matrix products: 12.6 us -> 5.6 us
    all_gather x1 -> x0, waiting for transfers between devices: 93.4 us -> none  [shards(): lax.all_gather(stacked, 'seq', axis=2, tiled=True)]
    pallas_call x0 -> x1, Pallas kernels: none -> 66.8 us  [project_keys(): pl.pallas_call(project_kernel, name='project', out_shape=(jax.ShapeDtypeS...]
    reduce_scatter x1 -> x0, waiting for transfers between devices: 41.9 us -> none  [shards(): lax.psum_scatter(partial_terms.astype(jnp.bfloat16), 'head', scatter_dime...]
    pallas_call x1, Pallas kernels: 38.7 us -> 31.3 us  [update_centroids(): pl.pallas_call(body, name='centroids', out_shape=(jax.ShapeDtypeStruct((r...]
    dot_general x1 -> x0, matrix products: 7.37 us -> none  [shards(): jnp.einsum('td,dkc->tkc', hidden_states, lax.all_gather(stacked, 'seq', a...]
  transfers between devices with their start and end apart: 2 -> 0, of which waited for: 2 -> 0; matrix products, arithmetic and copies ran while one was open for 1% -> 0% of each run, Pallas kernels for 0% -> 0%
where the time goes in v3:
time: 113 us; the launch traced here: 112 us
  Pallas kernels  98.1 us (87%)
  matrix products  5.6 us (5%)
  local copies, waits for them, and re-layouts  4.43 us (4%)
  other arithmetic  3.16 us (3%)
    pallas_call x1, Pallas kernels, project_keys(): pl.pallas_call(project_kernel, name='project', out_shape=(jax.ShapeDtypeS...  66.8 us
    pallas_call x1, Pallas kernels, update_centroids(): pl.pallas_call(body, name='centroids', out_shape=(jax.ShapeDtypeStruct((r...  31.3 us
    unnamed x13, local copies, waits for them, and re-layouts  2.99 us
    dot_general x1, matrix products, shards(): jnp.einsum('tc,te->ce', onehot.astype(jnp.bfloat16), keys, preferred_elem...  2.84 us
    dot_general x1, matrix products, shards(): jnp.einsum('te,ce->tc', keys, low, preferred_element_type=jnp.float32)  2.76 us

profile of v3, /device:TPU:1, one launch (start us, length us, event | category | flops | bytes accessed | tf_op | source)
XLA Modules:
  0.0 112.0 jit_solution(364139580744559589)
XLA Ops:
  0.6 0.0 copy-start
  0.6 0.0 copy-start.4
  0.7 1.0 copy-done
  1.7 0.6 dynamic-slice_bitcast_fusion.refs_2_
  2.3 1.4 %pad_maximum_fusion.w_ref = bf16[2,16,1024]{2,1,0:T(8,128)(2,1)} fusion(bf16[1,16,1024]{2,1,0:T(8,128)(2,1)} %bitcast.20, bf16[1,16,1024]{2,1,0:T(8,128)(2,1)} %bitcast.21), kind=kLoop, calls=%fused_computation.8 | loop fusion | flops 32768 | bytes 131072 | tf_op jit(solution)/shard_map/stack | solution.py:364
  3.7 66.8 %project.1 = (bf16[768,128]{1,0:T(8,128)(2,1)}, bf16[8,768,128]{2,1,0:T(8,128)(2,1)}) custom-call(bf16[768,1024]{1,0:T(8,128)(2,1)} %h_ref.1, bf16[2,16,1024]{2,1,0:T(8,128)(2,1)} %pad_maximum_fusion.w_ref), custom_call_target="tpu_custom_call" | custom-call | tf_op jit(solution)/shard_map/project/pallas_call | solution.py:220
  70.5 0.0 copy-done.4
  70.5 2.8 %fusion = f32[1024,128]{1,0:T(8,128)} fusion(bf16[768,128]{1,0:T(8,128)(2,1)} %get-tuple-element.18, s32[768]{0:T(1024)S(1)} %reduce.1), kind=kOutput, calls=%fused_computation.3 | convolution fusion | flops 202113024 | bytes 723968 | tf_op jit(solution)/shard_map/tc,te->ce/dot_general | solution.py:367
  73.4 0.0 copy-start.1
  73.4 0.4 convert_reduce_fusion
  73.7 0.1 reshape.24
  73.8 0.6 pad.4.refs_1_
  74.5 31.3 %centroids.1 = (f32[16,128]{1,0:T(8,128)}, bf16[32,2,16,128]{3,2,1,0:T(8,128)(2,1)}, bf16[768,128]{1,0:T(8,128)(2,1)}) custom-call(f32[32,2,16,128]{3,2,1,0:T(8,128)} %bitcast.17, f32[32,2,1,128]{3,2,1,0:T(1,128)} %pad.4.refs_1_, f32[16,128]{1,0:T(8,128)} %dynamic-slice_bitcast_fusion.refs_2_, bf16[8,768,128]{2,1,0:T(8,128)(2,1)} %get-tuple-element.10.refs_3_), custom_call_target="tpu_custom_call" | custom-call | tf_op jit(solution)/shard_map/centroids/pallas_call | solution.py:334
  105.8 1.2 %multiply_reduce_fusion = f32[32,2,16]{2,1,0:T(2,128)S(1)} fusion(bf16[32,2,16,128]{3,2,1,0:T(8,128)(2,1)} %get-tuple-element.13), kind=kLoop, calls=%fused_computation.6 | loop fusion | flops 392192 | bytes 266240 | tf_op jit(solution)/shard_map/reduce_sum | solution.py:382
  107.0 0.1 add.16
  107.1 0.0 copy-done.1
  107.1 0.2 multiply_reduce_fusion.1
  107.3 0.0 copy-start.2
  107.3 0.0 copy-start.3
  107.3 2.8 %fusion.2 = bf16[1,768,1024]{2,1,0:T(8,128)(2,1)} fusion(f32[1024]{0:T(1024)S(1)} %add.16, bf16[768,128]{1,0:T(8,128)(2,1)S(1)} %copy-done.1, bf16[1024,128]{1,0:T(8,128)(2,1)} %bitcast.18, f32[768]{0:T(1024)S(1)} %multiply_reduce_fusion.1), kind=kOutput, calls=%fused_computation.5 | convolution fusion | flops 205258752 | bytes 2038784 | tf_op jit(solution)/shard_map/te,ce->tc/dot_general | solution.py:385
  110.1 0.7 copy.14
  110.8 0.0 copy-done.2
  110.8 0.7 copy.15
  111.4 0.0 copy-done.3
  111.4 0.6 copy.16
  (1 shorter events, 0.0 us)
Async XLA Ops:
  0.6 1.0 copy-start
  0.6 69.8 %copy-start.4 = (s32[1,768]{1,0:T(1,128)S(1)}, s32[1,768]{1,0:T(1,128)}, u32[]{:S(2)}) copy-start(s32[1,768]{1,0:T(1,128)} %param.8) | copy-start | bytes 9220
  73.4 33.8 %copy-start.1 = (bf16[768,128]{1,0:T(8,128)(2,1)S(1)}, bf16[768,128]{1,0:T(8,128)(2,1)}, u32[]{:S(2)}) copy-start(bf16[768,128]{1,0:T(8,128)(2,1)} %get-tuple-element.18) | copy-start | bytes 589828
  107.3 3.5 %copy-start.2 = (bf16[768,128]{1,0:T(8,128)(2,1)S(1)}, bf16[768,128]{1,0:T(8,128)(2,1)}, u32[]{:S(2)}) copy-start(bf16[768,128]{1,0:T(8,128)(2,1)} %get-tuple-element.19) | copy-start | bytes 589828
  107.3 4.1 %copy-start.3 = (f32[16,128]{1,0:T(8,128)S(1)}, f32[16,128]{1,0:T(8,128)}, u32[]{:S(2)}) copy-start(f32[16,128]{1,0:T(8,128)} %get-tuple-element.12) | copy-start | bytes 24580

commit v4 on v3

--- a/solution.py
+++ b/solution.py
@@ -8,7 +8,7 @@
 MESH = pl.DeviceIdType.MESH
 NX, NY, NZ = 4, 8, 8
 CHIPS = NX * NY
-PIECES = 2
+PIECES = 3
 
 
 def remote(src, dst, send_sem, recv_sem, to):
@@ -140,7 +140,7 @@
         )
 
         def rows(i, carry):
-            at_rows = pl.ds(pl.multiple_of(i * 256, 256), 256)
+            at_rows = pl.ds(pl.multiple_of(i * 384, 384), 384)
             out = lax.dot_general(
                 h_ref[at_rows, :], weights, (((1,), (1,)), ((), ())),
                 preferred_element_type=jnp.float32,
@@ -149,7 +149,7 @@
                 parts[j][head, at_rows, :] = out[:, q * 128:(q + 1) * 128]
             return carry
 
-        lax.fori_loop(0, h_ref.shape[0] // 256, rows, 0)
+        lax.fori_loop(0, h_ref.shape[0] // 384, rows, 0)
 
     def first(j):
         for k in range(NX):
@@ -167,9 +167,13 @@
 
     half = NY // 2
 
-    def relay(j, s):
+    def pieces(s):
         ups = [k for k in range(NX) if s < half or k < NX // 2]
         downs = [k for k in range(NX) if s < half or k >= NX // 2]
+        return ups, downs
+
+    def relay(j, s):
+        ups, downs = pieces(s)
         for k in range(NX):
             if k in ups:
                 ref = block(j, y + NY - s, k)
@@ -183,6 +187,9 @@
                 if s < half - 1 or (s == half - 1 and k >= NX // 2):
                     push(j, ref, down(s + 1, k), below)
                 push(j, ref, side(down(s, k)), partner)
+
+    def use(j, s):
+        ups, downs = pieces(s)
         for k in ups:
             copy(j, block(j, y + NY - s, k, 1 - core), side(up(s, k)), partner).wait_recv()
         for k in downs:
@@ -200,16 +207,33 @@
             push(j, block(j, y, 0), 68 + k, x_peers[k - 1])
     first(0)
     mine(0)
-    for s in range(1, half + 1):
-        relay(0, s)
+    relay(0, 1)
+    relay(0, 2)
+    use(0, 1)
+    relay(0, 3)
+    first(1)
+    use(0, 2)
+    relay(0, 4)
+    use(0, 3)
+    use(0, 4)
     ring = Ring(pk, k_ref, plus, minus, zsend, zrecv, sent)
     ring.start()
-    first(1)
+    relay(1, 1)
     mine(1)
-    for s in range(NZ - 1):
-        ring.step(s)
-        if s in (0, 2, 4, 5):
-            relay(1, (0, 2, 4, 5).index(s) + 1)
+    ring.step(0)
+    relay(1, 2)
+    use(1, 1)
+    ring.step(1)
+    relay(1, 3)
+    ring.step(2)
+    use(1, 2)
+    ring.step(3)
+    relay(1, 4)
+    ring.step(4)
+    use(1, 3)
+    ring.step(5)
+    use(1, 4)
+    ring.step(6)
     for c in sent:
         c.wait_send()
 

time: 113 us -> 111 us (0.982)
  Pallas kernels: 98.1 us -> 96.9 us
    pallas_call x1, Pallas kernels: 66.8 us -> 61.2 us  [project_keys(): pl.pallas_call(project_kernel, name='project', out_shape=(jax.ShapeDtypeS...]
    pallas_call x1, Pallas kernels: 31.3 us -> 35.8 us  [update_centroids(): pl.pallas_call(body, name='centroids', out_shape=(jax.ShapeDtypeStruct((r...]
where the time goes in v4:
time: 111 us
  Pallas kernels  96.9 us (87%)
  matrix products  5.6 us (5%)
  local copies, waits for them, and re-layouts  4.43 us (4%)
  other arithmetic  3.16 us (3%)
    pallas_call x1, Pallas kernels, project_keys(): pl.pallas_call(project_kernel, name='project', out_shape=(jax.ShapeDtypeS...  61.2 us
    pallas_call x1, Pallas kernels, update_centroids(): pl.pallas_call(body, name='centroids', out_shape=(jax.ShapeDtypeStruct((r...  35.8 us
    unnamed x13, local copies, waits for them, and re-layouts  2.99 us
    dot_general x1, matrix products, shards(): jnp.einsum('tc,te->ce', onehot.astype(jnp.bfloat16), keys, preferred_elem...  2.84 us
    dot_general x1, matrix products, shards(): jnp.einsum('te,ce->tc', keys, low, preferred_element_type=jnp.float32)  2.76 us

profile of v4, /device:TPU:1, one launch (start us, length us, event | category | flops | bytes accessed | tf_op | source)
XLA Modules:
  0.0 110.9 jit_solution(10409580641368627821)
XLA Ops:
  0.6 0.0 copy-start
  0.6 0.0 copy-start.4
  0.7 1.0 copy-done
  1.7 0.6 dynamic-slice_bitcast_fusion.refs_2_
  2.3 1.4 %pad_maximum_fusion.w_ref = bf16[2,16,1024]{2,1,0:T(8,128)(2,1)} fusion(bf16[1,16,1024]{2,1,0:T(8,128)(2,1)} %bitcast.20, bf16[1,16,1024]{2,1,0:T(8,128)(2,1)} %bitcast.21), kind=kLoop, calls=%fused_computation.8 | loop fusion | flops 32768 | bytes 131072 | tf_op jit(solution)/shard_map/stack | solution.py:388
  3.7 61.2 %project.1 = (bf16[768,128]{1,0:T(8,128)(2,1)}, bf16[8,768,128]{2,1,0:T(8,128)(2,1)}) custom-call(bf16[768,1024]{1,0:T(8,128)(2,1)} %h_ref.1, bf16[2,16,1024]{2,1,0:T(8,128)(2,1)} %pad_maximum_fusion.w_ref), custom_call_target="tpu_custom_call" | custom-call | tf_op jit(solution)/shard_map/project/pallas_call | solution.py:244
  64.9 0.0 copy-done.4
  64.9 2.8 %fusion = f32[1024,128]{1,0:T(8,128)} fusion(bf16[768,128]{1,0:T(8,128)(2,1)} %get-tuple-element.18, s32[768]{0:T(1024)S(1)} %reduce.1), kind=kOutput, calls=%fused_computation.3 | convolution fusion | flops 202113024 | bytes 723968 | tf_op jit(solution)/shard_map/tc,te->ce/dot_general | solution.py:391
  67.7 0.0 copy-start.1
  67.7 0.4 convert_reduce_fusion
  68.1 0.1 reshape.24
  68.2 0.6 pad.4.refs_1_
  68.9 35.8 %centroids.1 = (f32[16,128]{1,0:T(8,128)}, bf16[32,2,16,128]{3,2,1,0:T(8,128)(2,1)}, bf16[768,128]{1,0:T(8,128)(2,1)}) custom-call(f32[32,2,16,128]{3,2,1,0:T(8,128)} %bitcast.17, f32[32,2,1,128]{3,2,1,0:T(1,128)} %pad.4.refs_1_, f32[16,128]{1,0:T(8,128)} %dynamic-slice_bitcast_fusion.refs_2_, bf16[8,768,128]{2,1,0:T(8,128)(2,1)} %get-tuple-element.10.refs_3_), custom_call_target="tpu_custom_call" | custom-call | tf_op jit(solution)/shard_map/centroids/pallas_call | solution.py:358
  104.7 1.2 %multiply_reduce_fusion = f32[32,2,16]{2,1,0:T(2,128)S(1)} fusion(bf16[32,2,16,128]{3,2,1,0:T(8,128)(2,1)} %get-tuple-element.13), kind=kLoop, calls=%fused_computation.6 | loop fusion | flops 392192 | bytes 266240 | tf_op jit(solution)/shard_map/reduce_sum | solution.py:406
  105.8 0.1 add.16
  105.9 0.0 copy-done.1
  105.9 0.2 multiply_reduce_fusion.1
  106.1 0.0 copy-start.2
  106.1 0.0 copy-start.3
  106.1 2.8 %fusion.2 = bf16[1,768,1024]{2,1,0:T(8,128)(2,1)} fusion(f32[1024]{0:T(1024)S(1)} %add.16, bf16[768,128]{1,0:T(8,128)(2,1)S(1)} %copy-done.1, bf16[1024,128]{1,0:T(8,128)(2,1)} %bitcast.18, f32[768]{0:T(1024)S(1)} %multiply_reduce_fusion.1), kind=kOutput, calls=%fused_computation.5 | convolution fusion | flops 205258752 | bytes 2038784 | tf_op jit(solution)/shard_map/te,ce->tc/dot_general | solution.py:409
  108.9 0.7 copy.14
  109.6 0.0 copy-done.2
  109.6 0.7 copy.15
  110.3 0.0 copy-done.3
  110.3 0.6 copy.16
  (1 shorter events, 0.0 us)
Async XLA Ops:
  0.6 1.0 copy-start
  0.6 64.2 %copy-start.4 = (s32[1,768]{1,0:T(1,128)S(1)}, s32[1,768]{1,0:T(1,128)}, u32[]{:S(2)}) copy-start(s32[1,768]{1,0:T(1,128)} %param.8) | copy-start | bytes 9220
  67.7 38.2 %copy-start.1 = (bf16[768,128]{1,0:T(8,128)(2,1)S(1)}, bf16[768,128]{1,0:T(8,128)(2,1)}, u32[]{:S(2)}) copy-start(bf16[768,128]{1,0:T(8,128)(2,1)} %get-tuple-element.18) | copy-start | bytes 589828
  106.1 3.5 %copy-start.2 = (bf16[768,128]{1,0:T(8,128)(2,1)S(1)}, bf16[768,128]{1,0:T(8,128)(2,1)}, u32[]{:S(2)}) copy-start(bf16[768,128]{1,0:T(8,128)(2,1)} %get-tuple-element.19) | copy-start | bytes 589828
  106.1 4.1 %copy-start.3 = (f32[16,128]{1,0:T(8,128)S(1)}, f32[16,128]{1,0:T(8,128)}, u32[]{:S(2)}) copy-start(f32[16,128]{1,0:T(8,128)} %get-tuple-element.12) | copy-start | bytes 24580

commit v5 on v4

--- a/solution.py
+++ b/solution.py
@@ -8,7 +8,7 @@
 MESH = pl.DeviceIdType.MESH
 NX, NY, NZ = 4, 8, 8
 CHIPS = NX * NY
-PIECES = 3
+PIECES = 2
 
 
 def remote(src, dst, send_sem, recv_sem, to):
@@ -209,9 +209,9 @@
     mine(0)
     relay(0, 1)
     relay(0, 2)
+    first(1)
     use(0, 1)
     relay(0, 3)
-    first(1)
     use(0, 2)
     relay(0, 4)
     use(0, 3)

time: 111 us -> 112 us (level)
  no operation moved by 1% of the time
where the time goes in v5:
time: 112 us; the launch traced here: 111 us
  Pallas kernels  97.3 us (87%)
  matrix products  5.61 us (5%)
  local copies, waits for them, and re-layouts  4.43 us (4%)
  other arithmetic  3.16 us (3%)
    pallas_call x1, Pallas kernels, project_keys(): pl.pallas_call(project_kernel, name='project', out_shape=(jax.ShapeDtypeS...  61.9 us
    pallas_call x1, Pallas kernels, update_centroids(): pl.pallas_call(body, name='centroids', out_shape=(jax.ShapeDtypeStruct((r...  35.3 us
    unnamed x13, local copies, waits for them, and re-layouts  2.99 us
    dot_general x1, matrix products, shards(): jnp.einsum('tc,te->ce', onehot.astype(jnp.bfloat16), keys, preferred_elem...  2.84 us
    dot_general x1, matrix products, shards(): jnp.einsum('te,ce->tc', keys, low, preferred_element_type=jnp.float32)  2.77 us

profile of v5, /device:TPU:1, one launch (start us, length us, event | category | flops | bytes accessed | tf_op | source)
XLA Modules:
  0.0 111.2 jit_solution(615176240839200014)
XLA Ops:
  0.6 0.0 copy-start
  0.6 0.0 copy-start.4
  0.7 1.0 copy-done
  1.7 0.6 dynamic-slice_bitcast_fusion.refs_2_
  2.3 1.4 %pad_maximum_fusion.w_ref = bf16[2,16,1024]{2,1,0:T(8,128)(2,1)} fusion(bf16[1,16,1024]{2,1,0:T(8,128)(2,1)} %bitcast.20, bf16[1,16,1024]{2,1,0:T(8,128)(2,1)} %bitcast.21), kind=kLoop, calls=%fused_computation.8 | loop fusion | flops 32768 | bytes 131072 | tf_op jit(solution)/shard_map/stack | solution.py:388
  3.7 61.9 %project.1 = (bf16[768,128]{1,0:T(8,128)(2,1)}, bf16[8,768,128]{2,1,0:T(8,128)(2,1)}) custom-call(bf16[768,1024]{1,0:T(8,128)(2,1)} %h_ref.1, bf16[2,16,1024]{2,1,0:T(8,128)(2,1)} %pad_maximum_fusion.w_ref), custom_call_target="tpu_custom_call" | custom-call | tf_op jit(solution)/shard_map/project/pallas_call | solution.py:244
  65.6 0.0 copy-done.4
  65.7 2.8 %fusion = f32[1024,128]{1,0:T(8,128)} fusion(bf16[768,128]{1,0:T(8,128)(2,1)} %get-tuple-element.18, s32[768]{0:T(1024)S(1)} %reduce.1), kind=kOutput, calls=%fused_computation.3 | convolution fusion | flops 202113024 | bytes 723968 | tf_op jit(solution)/shard_map/tc,te->ce/dot_general | solution.py:391
  68.5 0.0 copy-start.1
  68.5 0.4 convert_reduce_fusion
  68.9 0.1 reshape.24
  69.0 0.6 pad.4.refs_1_
  69.6 35.3 %centroids.1 = (f32[16,128]{1,0:T(8,128)}, bf16[32,2,16,128]{3,2,1,0:T(8,128)(2,1)}, bf16[768,128]{1,0:T(8,128)(2,1)}) custom-call(f32[32,2,16,128]{3,2,1,0:T(8,128)} %bitcast.17, f32[32,2,1,128]{3,2,1,0:T(1,128)} %pad.4.refs_1_, f32[16,128]{1,0:T(8,128)} %dynamic-slice_bitcast_fusion.refs_2_, bf16[8,768,128]{2,1,0:T(8,128)(2,1)} %get-tuple-element.10.refs_3_), custom_call_target="tpu_custom_call" | custom-call | tf_op jit(solution)/shard_map/centroids/pallas_call | solution.py:358
  105.0 1.2 %multiply_reduce_fusion = f32[32,2,16]{2,1,0:T(2,128)S(1)} fusion(bf16[32,2,16,128]{3,2,1,0:T(8,128)(2,1)} %get-tuple-element.13), kind=kLoop, calls=%fused_computation.6 | loop fusion | flops 392192 | bytes 266240 | tf_op jit(solution)/shard_map/reduce_sum | solution.py:406
  106.1 0.1 add.16
  106.2 0.0 copy-done.1
  106.2 0.2 multiply_reduce_fusion.1
  106.4 0.0 copy-start.2
  106.4 0.0 copy-start.3
  106.5 2.8 %fusion.2 = bf16[1,768,1024]{2,1,0:T(8,128)(2,1)} fusion(f32[1024]{0:T(1024)S(1)} %add.16, bf16[768,128]{1,0:T(8,128)(2,1)S(1)} %copy-done.1, bf16[1024,128]{1,0:T(8,128)(2,1)} %bitcast.18, f32[768]{0:T(1024)S(1)} %multiply_reduce_fusion.1), kind=kOutput, calls=%fused_computation.5 | convolution fusion | flops 205258752 | bytes 2038784 | tf_op jit(solution)/shard_map/te,ce->tc/dot_general | solution.py:409
  109.2 0.7 copy.14
  109.9 0.0 copy-done.2
  109.9 0.7 copy.15
  110.6 0.0 copy-done.3
  110.6 0.6 copy.16
  (1 shorter events, 0.0 us)
Async XLA Ops:
  0.6 1.0 copy-start
  0.6 65.0 %copy-start.4 = (s32[1,768]{1,0:T(1,128)S(1)}, s32[1,768]{1,0:T(1,128)}, u32[]{:S(2)}) copy-start(s32[1,768]{1,0:T(1,128)} %param.8) | copy-start | bytes 9220
  68.5 37.7 %copy-start.1 = (bf16[768,128]{1,0:T(8,128)(2,1)S(1)}, bf16[768,128]{1,0:T(8,128)(2,1)}, u32[]{:S(2)}) copy-start(bf16[768,128]{1,0:T(8,128)(2,1)} %get-tuple-element.18) | copy-start | bytes 589828
  106.4 3.5 %copy-start.2 = (bf16[768,128]{1,0:T(8,128)(2,1)S(1)}, bf16[768,128]{1,0:T(8,128)(2,1)}, u32[]{:S(2)}) copy-start(bf16[768,128]{1,0:T(8,128)(2,1)} %get-tuple-element.19) | copy-start | bytes 589828
  106.4 4.1 %copy-start.3 = (f32[16,128]{1,0:T(8,128)S(1)}, f32[16,128]{1,0:T(8,128)}, u32[]{:S(2)}) copy-start(f32[16,128]{1,0:T(8,128)} %get-tuple-element.12) | copy-start | bytes 24580
